TPU v7x, 32 devices: a whole 2x2x4 slice. The times are simulated.
32 devices in a mesh: kv: 2 (over y), ctx: 16 (over z, x, core).
Axes of the slice: x: 2, y: 2, z: 4, core: 2. Of those that a mesh axis runs over, the one named last changes fastest.
Arguments:
- residual: bfloat16 [64, 8192], P(None, 'ctx'), may hold values from -8 to 8
- queries: bfloat16 [64, 8192], P(None, 'kv'), may hold values from -16 to 16
- draft_token_keys: bfloat16 [64, 1024], P(None, 'kv'), may hold values from -32 to 32
- draft_token_values: bfloat16 [64, 1024], P(None, 'kv'), may hold values from -8 to 8
- cache_keys: bfloat16 [2, 8192, 1024], P(None, 'ctx', 'kv'), may hold values from -32 to 32
- cached_value_rows: bfloat16 [2, 8192, 1024], P(None, 'ctx', 'kv'), may hold values from -8 to 8
- tenant_ids: int32 [64], replicated, may hold values from 0 to 1, as said below
- tree_mask: int32 [64, 64], replicated, may hold values from 0 to 1, as said below
- cache_lengths: int32 [2], replicated, may hold values from 4097 to 8192
- out_weight: bfloat16 [8192, 8192], P('kv', 'ctx'), may hold values from -0.0625 to 0.0625
- out_signs: bfloat16 [2, 8192, 8192], P(None, 'kv', 'ctx'), may hold values from -1 to 1, as said below
- norm_gain: float32 [8192], P('ctx'), may hold values from 0.1 to 1.9
- gate_weight: bfloat16 [8192, 16384], P(None, ('kv', 'ctx')), may hold values from -0.0625 to 0.0625
- up_weight: bfloat16 [8192, 16384], P(None, ('kv', 'ctx')), may hold values from -0.0625 to 0.0625
- down_weight: bfloat16 [16384, 8192], P(('kv', 'ctx')), may hold values from -0.09375 to 0.09375
- gate_signs: bfloat16 [2, 8192, 16384], P(None, None, ('kv', 'ctx')), may hold values from -1 to 1, as said below
- up_signs: bfloat16 [2, 8192, 16384], P(None, None, ('kv', 'ctx')), may hold values from -1 to 1, as said below
- down_signs: bfloat16 [2, 16384, 8192], P(None, ('kv', 'ctx')), may hold values from -1 to 1, as said below
- delta_scale: float32 [2, 4], replicated, may hold values from 0.3 to 0.9
Outputs:
- mixed: bfloat16 [64, 8192], P(None, 'ctx')
Inputs may be any that keep to these rules, and one draw needn't show every extreme that they name: `tenant_ids`: exactly 32 tokens belong to each tenant. `tree_mask`: entry (i, j) is 1 exactly when token j is token i or an ancestor of token i in the draft tree of their common tenant; each tenant's 32 tokens form one tree. `out_signs`: every entry is 1 or -1. `gate_signs`: every entry is 1 or -1. `up_signs`: every entry is 1 or -1. `down_signs`: every entry is 1 or -1.
All inputs are finite; a program needn't handle non-finite values.
Results may differ from a plain program's by a relative error of at most 0.013.
Values may be sent and summed in bfloat16 or wider, within the bound.
No kernel may reach another device: no remote copies, remote signals or barrier semaphores. Data moves between devices by JAX's collectives and lax.ppermute only.
A program may use at most 192 MiB of HBM per device.

v0:
```python
import jax
import jax.numpy as jnp
from jax import lax
from jax.sharding import PartitionSpec as P

D = 8192
QUERY_HEADS = 64
HEAD_SIZE = 128
FF = 16384
NEG = -1e30
EPS = 1e-05


def combine(first, second):
    first_top, first_total, first_out = first
    second_top, second_total, second_out = second
    peak = jnp.maximum(first_top, second_top)
    first_scale = jnp.exp(first_top - peak)
    second_scale = jnp.exp(second_top - peak)
    total = first_total * first_scale + second_total * second_scale
    merged = first_out * first_scale[..., None] + second_out * second_scale[..., None]
    return (peak, total, merged)


def draft_rows(query_rows, group_rows, visible_rows, key_rows, value_rows, factor):
    groups = key_rows.shape[1]
    choose = (group_rows[:, None] == jnp.arange(groups, dtype=jnp.int32)[None, :]).astype(
        jnp.float32
    )
    every_group = (
        jnp.einsum("rd,kgd->rgk", query_rows, key_rows, preferred_element_type=jnp.float32) * factor
    )
    scores = jnp.einsum("rgk,rg->rk", every_group, choose, precision=lax.Precision.HIGHEST)
    masked = jnp.where(visible_rows, scores, NEG)
    peak = jnp.max(masked, axis=-1)
    weights = jnp.where(visible_rows, jnp.exp(masked - peak[:, None]), 0.0)
    total = jnp.sum(weights, axis=-1)
    every_value = jnp.einsum(
        "rk,kgd->rgd", weights.astype(jnp.bfloat16), value_rows, preferred_element_type=jnp.float32
    )
    result = jnp.einsum("rgd,rg->rd", every_value, choose, precision=lax.Precision.HIGHEST)
    return (peak, total, result)


def shards(
    residual,
    queries,
    draft_token_keys,
    draft_token_values,
    cache_keys,
    cached_value_rows,
    tenant_ids,
    tree_mask,
    cache_lengths,
    out_weight,
    out_signs,
    norm_gain,
    gate_weight,
    up_weight,
    down_weight,
    gate_signs,
    up_signs,
    down_signs,
    delta_scale,
):
    tenants = cache_keys.shape[0]
    tokens = tenant_ids.shape[0]
    draft = tokens // tenants
    heads_here = queries.shape[1] // HEAD_SIZE
    groups_here = draft_token_keys.shape[1] // HEAD_SIZE
    group_width = heads_here // groups_here
    ctx_rows = cache_keys.shape[1]
    factor = HEAD_SIZE ** (-0.5)
    sort_order = jnp.argsort(tenant_ids, stable=True)
    inverse = jnp.argsort(sort_order)
    sorted_queries = queries[sort_order]
    query_blocks = sorted_queries.reshape(tenants, draft, groups_here, group_width, HEAD_SIZE)
    draft_key_lines = draft_token_keys[sort_order].reshape(tokens, groups_here, HEAD_SIZE)
    draft_value_lines = draft_token_values[sort_order].reshape(tokens, groups_here, HEAD_SIZE)
    visible = tree_mask[sort_order][:, sort_order] > 0
    first_slot = lax.axis_index("ctx") * ctx_rows
    slot_ids = first_slot + jnp.arange(ctx_rows, dtype=jnp.int32)
    live = (slot_ids[None, :] < cache_lengths[:, None])[:, None, None, None, :]
    cache_key_blocks = cache_keys.reshape(tenants, ctx_rows, groups_here, HEAD_SIZE)
    cache_value_blocks = cached_value_rows.reshape(tenants, ctx_rows, groups_here, HEAD_SIZE)
    scores = (
        jnp.einsum(
            "tqgwd,tjgd->tqgwj", query_blocks, cache_key_blocks, preferred_element_type=jnp.float32
        )
        * factor
    )
    masked = jnp.where(live, scores, NEG)
    peak = jnp.max(masked, axis=-1)
    weights = jnp.where(live, jnp.exp(masked - peak[..., None]), 0.0)
    total = jnp.sum(weights, axis=-1)
    weighted = jnp.einsum(
        "tqgwj,tjgd->tqgwd",
        weights.astype(jnp.bfloat16),
        cache_value_blocks,
        preferred_element_type=jnp.float32,
    )
    part_top = peak.reshape(tokens, heads_here)
    part_total = total.reshape(tokens, heads_here)
    part_out = weighted.reshape(tokens, heads_here, HEAD_SIZE)
    n_ctx = lax.axis_size("ctx")
    all_rows = tokens * heads_here
    share = all_rows // n_ctx
    got_top, got_total, got_out = (
        lax.all_to_all(
            part_top.reshape(1, all_rows), "ctx", split_axis=1, concat_axis=0, tiled=True
        ),
        lax.all_to_all(
            part_total.reshape(1, all_rows), "ctx", split_axis=1, concat_axis=0, tiled=True
        ),
        lax.all_to_all(
            part_out.reshape(1, all_rows, HEAD_SIZE), "ctx", split_axis=1, concat_axis=0, tiled=True
        ),
    )
    summit = jnp.max(got_top, axis=0)
    rescale = jnp.exp(got_top - summit)
    merged = (
        summit,
        jnp.sum(got_total * rescale, axis=0),
        jnp.sum(got_out * rescale[..., None], axis=0),
    )
    first_row = lax.axis_index("ctx") * share
    row_ids = first_row + jnp.arange(share, dtype=jnp.int32)
    token_rows = row_ids // heads_here
    group_rows = row_ids % heads_here // group_width
    query_rows = lax.dynamic_slice_in_dim(
        sorted_queries.reshape(all_rows, HEAD_SIZE), first_row, share, 0
    )
    own = draft_rows(
        query_rows, group_rows, visible[token_rows], draft_key_lines, draft_value_lines, factor
    )
    final_top, final_total, final_out = combine(merged, own)
    finished = (final_out / final_total[:, None]).astype(jnp.bfloat16)
    attention = lax.all_gather(finished, "ctx", axis=0, tiled=True).reshape(
        tokens, heads_here * HEAD_SIZE
    )
    attention_split = attention.reshape(tenants, draft, -1)
    projected = jnp.dot(attention, out_weight, preferred_element_type=jnp.float32)
    out_delta = jnp.einsum(
        "tqh,thf->tqf", attention_split, out_signs, preferred_element_type=jnp.float32
    )
    projected = projected + (
        out_delta * (delta_scale[:, 0] * (QUERY_HEADS * HEAD_SIZE) ** (-0.5))[:, None, None]
    ).reshape(tokens, -1)
    summed_heads = lax.psum(projected.astype(jnp.bfloat16), "kv").astype(jnp.float32)
    hidden = residual[sort_order].astype(jnp.float32) + summed_heads
    squares = lax.psum(jnp.sum(hidden * hidden, axis=1), "ctx")
    normed = (hidden * lax.rsqrt(squares / D + EPS)[:, None] * norm_gain).astype(jnp.bfloat16)
    hidden_units = gate_weight.shape[1]
    piece = lax.all_gather(normed, "ctx", axis=1, tiled=True)
    size = piece.shape[1]
    split_piece = piece.reshape(tenants, draft, size)
    gate_base = jnp.dot(piece, gate_weight, preferred_element_type=jnp.float32)
    up_base = jnp.dot(piece, up_weight, preferred_element_type=jnp.float32)
    gate_delta = jnp.einsum(
        "tqf,tfh->tqh", split_piece, gate_signs, preferred_element_type=jnp.float32
    )
    up_delta = jnp.einsum("tqf,tfh->tqh", split_piece, up_signs, preferred_element_type=jnp.float32)
    gate = gate_base + (gate_delta * (delta_scale[:, 1] * D ** (-0.5))[:, None, None]).reshape(
        tokens, hidden_units
    )
    up_part = up_base + (up_delta * (delta_scale[:, 2] * D ** (-0.5))[:, None, None]).reshape(
        tokens, hidden_units
    )
    active = (jax.nn.silu(gate) * up_part).astype(jnp.bfloat16)
    active_split = active.reshape(tenants, draft, hidden_units)
    down_factor = delta_scale[:, 3] * FF ** (-0.5)
    features_here = residual.shape[1]
    base_part = lax.dot_general(
        down_weight, active, (((0,), (1,)), ((), ())), preferred_element_type=jnp.float32
    )
    delta_part = jnp.einsum(
        "thf,tqh->ftq", down_signs, active_split, preferred_element_type=jnp.float32
    )
    delta_part = delta_part * down_factor[None, :, None]
    lowered = lax.psum_scatter(
        base_part + delta_part.reshape(features_here * lax.axis_size("ctx"), tokens),
        "ctx",
        scatter_dimension=0,
        tiled=True,
    )
    lowered = lax.psum(lowered.astype(jnp.bfloat16), "kv").astype(jnp.float32)
    return (hidden + lowered.T).astype(jnp.bfloat16)[inverse]


def solution(mesh):
    return jax.shard_map(
        shards,
        mesh=mesh,
        in_specs=(
            P(None, "ctx"),
            P(None, "kv"),
            P(None, "kv"),
            P(None, "kv"),
            P(None, "ctx", "kv"),
            P(None, "ctx", "kv"),
            P(),
            P(),
            P(),
            P("kv", "ctx"),
            P(None, "kv", "ctx"),
            P("ctx"),
            P(None, ("kv", "ctx")),
            P(None, ("kv", "ctx")),
            P(("kv", "ctx"), None),
            P(None, None, ("kv", "ctx")),
            P(None, None, ("kv", "ctx")),
            P(None, ("kv", "ctx"), None),
            P(),
        ),
        out_specs=P(None, "ctx"),
        check_vma=False,
    )
```

profile of v0, /device:TPU:0, one launch (start us, length us, event | category | flops | bytes accessed | tf_op | source)
XLA Modules:
  0.0 308.4 jit_solution(11207596414709739598)
XLA Ops:
  6.5 2.8 sort.34
  11.7 1.9 copy-done.3
  15.7 7.4 %all-to-all-start.2 = ((f32[1,16,128]{2,0,1:T(1,128)}), f32[1,16,128]{2,0,1:T(1,128)S(1)}, u32[]{:S(2)}, u32[]{:S(2)}) async-start(f32[1,16,128]{2,0,1:T(1,128)} %bitcast.17), calls=%async_computation.2 | async-start | bytes 16384 | tf_op jit(solution)/shard_map/all_to_all | solution.py:112
  24.2 3.6 %fusion.9 = f32[2,32,4,8,128]{4,3,1,2,0:T(8,128)S(1)} fusion(f32[2,4,32,8,512]{4,3,2,1,0:T(8,128)} %copy-done.3, f32[2,32,4,8]{3,1,2,0:T(8,128)S(1)} %get-tuple-element.20, pred[2,512]{1,0:T(4,128)(4,1)S(1)} %broadcast_compare_fusion, bf16[2,512,4,128,1]{3,2,1,0,4:T(4,128)(2,1)} %bitcast.112), kind=kOutput, calls=%fused_computation.21 | convolution fusion | flops 273678336 | bytes 6300672 | tf_op jit(solution)/shard_map/tqgwj,tjgd->tqgwd/dot_general | solution.py:96
  29.4 5.2 %all-to-all-start.1 = ((f32[1,16,128]{2,0,1:T(1,128)}), f32[1,16,128]{2,0,1:T(1,128)S(1)}, u32[]{:S(2)}, u32[]{:S(2)}) async-start(f32[1,16,128]{2,0,1:T(1,128)} %bitcast.7), calls=%async_computation.1 | async-start | bytes 16384 | tf_op jit(solution)/shard_map/all_to_all | solution.py:109
  36.1 5.0 %all-to-all-done.1 = f32[1,16,128]{2,0,1:T(1,128)S(1)} async-done(((f32[1,16,128]{2,0,1:T(1,128)}), f32[1,16,128]{2,0,1:T(1,128)S(1)}, u32[]{:S(2)}, u32[]{:S(2)}) %all-to-all-start.1) | async-done | bytes 8224 | tf_op jit(solution)/shard_map/all_to_all | solution.py:109
  41.1 3.7 %all-to-all-start = ((f32[1,2048,128]{2,0,1:T(1,128)}), f32[1,2048,128]{2,0,1:T(1,128)S(1)}, u32[]{:S(2)}, u32[]{:S(2)}) async-start(f32[1,2048,128]{2,0,1:T(1,128)} %bitcast.5), calls=%async_computation | async-start | bytes 2097152 | tf_op jit(solution)/shard_map/all_to_all | solution.py:115
  50.1 17.5 %all-to-all-done = f32[1,2048,128]{2,0,1:T(1,128)S(1)} async-done(((f32[1,2048,128]{2,0,1:T(1,128)}), f32[1,2048,128]{2,0,1:T(1,128)S(1)}, u32[]{:S(2)}, u32[]{:S(2)}) %all-to-all-start) | async-done | bytes 1048608 | tf_op jit(solution)/shard_map/all_to_all | solution.py:115
  68.1 24.0 %all_gather.6 = bf16[2048,128]{1,0:T(8,128)(2,1)S(1)} all-gather(bf16[128,128]{1,0:T(8,128)(2,1)S(1)} %divide_convert_fusion), channel_id=1, replica_groups=mesh['kv'=2,'ctx'=16] {'ctx'}, dimensions={0}, use_global_device_ids=true | all-gather | bytes 557056 | tf_op jit(solution)/shard_map/all_gather | solution.py:138
  92.6 5.1 %convolution_multiply_fusion.1 = f32[2,32,512]{2,1,0:T(8,128)S(1)} fusion(bf16[2,32,4096]{2,1,0:T(8,128)(2,1)S(1)} %reshape_reshape.9, bf16[2,4096,512]{2,1,0:T(8,128)(2,1)} %param.29, f32[2]{0:T(128)S(1)} %get-tuple-element.11), kind=kOutput, calls=%fused_computation.22 | convolution fusion | flops 268468224 | bytes 9043976 | tf_op jit(solution)/shard_map/tqh,thf->tqf/dot_general | solution.py:143
  99.9 17.6 %all-reduce.3.cloned.1.call-done = bf16[64,512]{1,0:T(8,128)(2,1)} async-done(((bf16[64,512]{1,0:T(8,128)(2,1)}), bf16[64,512]{1,0:T(8,128)(2,1)}) %all-reduce.3.cloned.1.call-update) | async-done | bytes 65552 | tf_op jit(solution)/shard_map/psum | solution.py:149
  118.5 32.7 %psum.22 = f32[64]{0:T(128)S(1)} all-reduce(f32[64]{0:T(128)S(1)} %multiply_reduce_fusion.1), channel_id=1, replica_groups=mesh['kv'=2,'ctx'=16] {'ctx'}, use_global_device_ids=true, to_apply=%region_10.11 | all-reduce | flops 64 | bytes 512 | tf_op jit(solution)/shard_map/psum | solution.py:151
  151.2 1.6 multiply_convert_fusion
  153.0 32.9 %all-gather.2.cloned.1.call-done = bf16[64,8192]{1,0:T(8,128)(2,1)} async-done(((bf16[64,512]{1,0:T(8,128)(2,1)}), bf16[64,8192]{1,0:T(8,128)(2,1)}) %all-gather.2.cloned.1.call-update) | async-done | bytes 1048592 | tf_op jit(solution)/shard_map/all_gather | solution.py:154
  185.9 9.1 %convolution_multiply_fusion.3 = f32[2,32,512]{2,1,0:T(8,128)S(1)} fusion(bf16[2,32,8192]{2,1,0:T(8,128)(2,1)} %bitcast.93, bf16[2,8192,512]{2,1,0:T(8,128)(2,1)} %param.34, f32[2]{0:T(128)S(1)} %get-tuple-element.10), kind=kOutput, calls=%fused_computation.27 | convolution fusion | flops 536903680 | bytes 17956872 | tf_op jit(solution)/shard_map/tqf,tfh->tqh/dot_general | solution.py:159
  195.1 8.8 %convolution_multiply_fusion.2 = f32[2,32,512]{2,1,0:T(8,128)S(1)} fusion(bf16[2,32,8192]{2,1,0:T(8,128)(2,1)S(1)} %bitcast.94, bf16[2,8192,512]{2,1,0:T(8,128)(2,1)} %param.35, f32[2]{0:T(128)S(1)} %get-tuple-element.12), kind=kOutput, calls=%fused_computation.24 | convolution fusion | flops 536903680 | bytes 17956872 | tf_op jit(solution)/shard_map/tqf,tfh->tqh/dot_general | solution.py:162
  204.0 1.6 convolution_add_fusion.2
  205.7 1.6 fusion.15
  210.1 3.0 convolution_multiply_fusion
  213.1 2.9 fusion
  216.1 2.0 sort.35
  218.1 59.5 %reduce-scatter.2.cloned.1.call-done = f32[512,64]{0,1:T(8,128)} async-done(((f32[8192,64]{0,1:T(8,128)}), f32[512,64]{0,1:T(8,128)}) %reduce-scatter.2.cloned.1.call-update) | async-done | bytes 131088 | tf_op jit(solution)/shard_map/reduce_scatter | solution.py:180
  277.7 1.5 convert_bitcast_fusion
  279.3 20.4 %all-reduce.5.cloned.1.call-done = bf16[64,512]{1,0:T(8,128)(2,1)} async-done(((bf16[64,512]{1,0:T(8,128)(2,1)}), bf16[64,512]{1,0:T(8,128)(2,1)}) %all-reduce.5.cloned.1.call-update) | async-done | bytes 65552 | tf_op jit(solution)/shard_map/psum | solution.py:186
  (115 shorter events, 23.4 us)
Async XLA Ops:
  10.7 12.3 %copy-start.10 = (bf16[2,512,512]{2,1,0:T(8,128)(2,1)S(1)}, bf16[2,512,512]{2,1,0:T(8,128)(2,1)}, u32[]{:S(2)}) copy-start(bf16[2,512,512]{2,1,0:T(8,128)(2,1)} %param.24) | copy-start | bytes 3145732
  15.7 13.8 %all-to-all-start.2 = ((f32[1,16,128]{2,0,1:T(1,128)}), f32[1,16,128]{2,0,1:T(1,128)S(1)}, u32[]{:S(2)}, u32[]{:S(2)}) async-start(f32[1,16,128]{2,0,1:T(1,128)} %bitcast.17), calls=%async_computation.2 | async-start | bytes 16384 | tf_op jit(solution)/shard_map/all_to_all | solution.py:112
  27.8 17.2 %copy-start.5 = (bf16[64,512]{1,0:T(8,128)(2,1)S(1)}, bf16[64,512]{1,0:T(8,128)(2,1)}, u32[]{:S(2)}) copy-start(bf16[64,512]{1,0:T(8,128)(2,1)} %param.21) | copy-start | bytes 196612
  27.8 17.9 %copy-start.8 = (s32[64,64]{1,0:T(8,128)S(1)}, s32[64,64]{1,0:T(8,128)}, u32[]{:S(2)}) copy-start(s32[64,64]{1,0:T(8,128)} %param.26) | copy-start | bytes 49156
  27.8 20.1 %copy-start.6 = (bf16[64,512]{1,0:T(8,128)(2,1)S(1)}, bf16[64,512]{1,0:T(8,128)(2,1)}, u32[]{:S(2)}) copy-start(bf16[64,512]{1,0:T(8,128)(2,1)} %param.22) | copy-start | bytes 196612
  27.8 20.8 %copy-start.12 = (f32[2,4]{1,0:T(2,128)S(1)}, f32[2,4]{1,0:T(2,128)}, u32[]{:S(2)}) copy-start(f32[2,4]{1,0:T(2,128)} %param.37) | copy-start | bytes 100
  29.4 11.7 %all-to-all-start.1 = ((f32[1,16,128]{2,0,1:T(1,128)}), f32[1,16,128]{2,0,1:T(1,128)S(1)}, u32[]{:S(2)}, u32[]{:S(2)}) async-start(f32[1,16,128]{2,0,1:T(1,128)} %bitcast.7), calls=%async_computation.1 | async-start | bytes 16384 | tf_op jit(solution)/shard_map/all_to_all | solution.py:109
  41.1 26.5 %all-to-all-start = ((f32[1,2048,128]{2,0,1:T(1,128)}), f32[1,2048,128]{2,0,1:T(1,128)S(1)}, u32[]{:S(2)}, u32[]{:S(2)}) async-start(f32[1,2048,128]{2,0,1:T(1,128)} %bitcast.5), calls=%async_computation | async-start | bytes 2097152 | tf_op jit(solution)/shard_map/all_to_all | solution.py:115
  44.8 72.7 %all-reduce.3.cloned.1.call-start = ((), (), s32[]{:S(2)}) async-start(), calls=%async_computation.4 | async-start | bytes 131072 | tf_op jit(solution)/shard_map/psum | solution.py:149
  92.5 5.1 %copy-start.4 = (bf16[4096,512]{1,0:T(8,128)(2,1)S(1)}, bf16[4096,512]{1,0:T(8,128)(2,1)}, u32[]{:S(2)}) copy-start(bf16[4096,512]{1,0:T(8,128)(2,1)} %param.28) | copy-start | bytes 12582916
  97.6 53.6 %copy-start.13 = (f32[512]{0:T(512)S(1)}, f32[512]{0:T(512)}, u32[]{:S(2)}) copy-start(f32[512]{0:T(512)} %param.30) | copy-start | bytes 6148
  99.1 86.8 %all-gather.2.cloned.1.call-start = ((), (), s32[]{:S(2)}) async-start(), calls=%async_computation.5 | async-start | bytes 1114112 | tf_op jit(solution)/shard_map/all_gather | solution.py:154
  152.8 124.9 %reduce-scatter.2.cloned.1.call-start = ((), (), s32[]{:S(2)}) async-start(), calls=%async_computation.6 | async-start | bytes 2228224 | tf_op jit(solution)/shard_map/reduce_scatter | solution.py:180
  185.9 9.2 %copy-start.2 = (bf16[64,8192]{1,0:T(8,128)(2,1)S(1)}, bf16[64,8192]{1,0:T(8,128)(2,1)}, u32[]{:S(2)}) copy-start(bf16[64,8192]{1,0:T(8,128)(2,1)} %all-gather.2.cloned.1.call-done) | copy-start | bytes 3145732
  185.9 18.1 %slice-start = ((s8[8388608]{0:T(1024)(128)(4,1)}), s8[4194304]{0:T(1024)(128)(4,1)S(1)}, s32[]{:S(2)}) async-start(s8[8388608]{0:T(1024)(128)(4,1)} %bitcast.95), calls=%async_computation.8 | async-start | bytes 8388608
  185.9 19.7 %slice-start.2 = ((s8[8388608]{0:T(1024)(128)(4,1)}), s8[4194304]{0:T(1024)(128)(4,1)S(1)}, s32[]{:S(2)}) async-start(s8[8388608]{0:T(1024)(128)(4,1)} %bitcast.97), calls=%async_computation.10 | async-start | bytes 8388608
  195.1 8.9 %slice-start.1 = ((s8[8388608]{0:T(1024)(128)(4,1)}), s8[4194304]{0:T(1024)(128)(4,1)S(1)}, s32[]{:S(2)}) async-start(s8[8388608]{0:T(1024)(128)(4,1)} %bitcast.95), calls=%async_computation.9 | async-start | bytes 8388608
  195.1 10.5 %slice-start.3 = ((s8[8388608]{0:T(1024)(128)(4,1)}), s8[4194304]{0:T(1024)(128)(4,1)S(1)}, s32[]{:S(2)}) async-start(s8[8388608]{0:T(1024)(128)(4,1)} %bitcast.97), calls=%async_computation.11 | async-start | bytes 8388608
  204.0 4.6 %slice-start.8 = ((s8[16777216]{0:T(1024)(128)(4,1)}), s8[4194304]{0:T(1024)(128)(4,1)S(1)}, s32[]{:S(2)}) async-start(s8[16777216]{0:T(1024)(128)(4,1)} %bitcast.102), calls=%async_computation.16 | async-start | bytes 8388608
  205.6 4.4 %slice-start.9 = ((s8[16777216]{0:T(1024)(128)(4,1)}), s8[4194304]{0:T(1024)(128)(4,1)S(1)}, s32[]{:S(2)}) async-start(s8[16777216]{0:T(1024)(128)(4,1)} %bitcast.102), calls=%async_computation.17 | async-start | bytes 8388608
  205.6 7.4 %slice-start.4 = ((s8[8388608]{0:T(1024)(128)(4,1)}), s8[4194304]{0:T(1024)(128)(4,1)S(1)}, s32[]{:S(2)}) async-start(s8[8388608]{0:T(1024)(128)(4,1)} %bitcast.99), calls=%async_computation.12 | async-start | bytes 8388608
  213.1 86.6 %copy-start.11 = (bf16[64,512]{1,0:T(8,128)(2,1)S(1)}, bf16[64,512]{1,0:T(8,128)(2,1)}, u32[]{:S(2)}) copy-start(bf16[64,512]{1,0:T(8,128)(2,1)} %all-reduce.3.cloned.1.call-done) | copy-start | bytes 196612
  213.1 88.8 %copy-start.1 = (bf16[64,4096]{1,0:T(8,128)(2,1)S(1)}, bf16[64,4096]{1,0:T(8,128)(2,1)}, u32[]{:S(2)}) copy-start(bf16[64,4096]{1,0:T(8,128)(2,1)} %param.20) | copy-start | bytes 1572868
  216.1 83.7 %all-reduce.5.cloned.1.call-start = ((), (), s32[]{:S(2)}) async-start(), calls=%async_computation.7 | async-start | bytes 131072 | tf_op jit(solution)/shard_map/psum | solution.py:186
  (8 other events, 24.0 us)
Sparse Core Ops, SparseCore 0:
  99.3 18.2 all-reduce.2
  152.9 32.9 all-gather.1
  216.2 61.4 reduce-scatter.1
  279.8 19.8 all-reduce.4
where the time goes:
time: 309 us; the launch traced here: 308 us
  waiting for transfers between devices  154 us (50%)
  blocking collectives  56.7 us (18%)
  matrix products  39 us (13%)
  starting transfers between devices  16.6 us (5%)
  local copies, waits for them, and re-layouts  16.5 us (5%)
  between operations  13.7 us (4%)
  other arithmetic  12.1 us (4%)
    reduce_scatter x1, waiting for transfers between devices, shards(): lax.psum_scatter(base_part + delta_part.reshape(features_here * lax.axis_...  59.5 us
    all_gather x1, waiting for transfers between devices, shards(): piece = lax.all_gather(normed, 'ctx', axis=1, tiled=True)  32.9 us
    psum x1, blocking collectives, shards(): squares = lax.psum(jnp.sum(hidden * hidden, axis=1), 'ctx')  32.7 us
    all_gather x1, blocking collectives, shards(): lax.all_gather(finished, 'ctx', axis=0, tiled=True)  24 us
    psum x1, waiting for transfers between devices, shards(): lowered = lax.psum(lowered.astype(jnp.bfloat16), 'kv').astype(jnp.float32)  20.4 us
    psum x1, waiting for transfers between devices, shards(): lax.psum(projected.astype(jnp.bfloat16), 'kv').astype(jnp.float32)  17.6 us
    all_to_all x1, waiting for transfers between devices, shards(): lax.all_to_all(part_out.reshape(1, all_rows, HEAD_SIZE), 'ctx', split_axi...  17.5 us
    dot_general x1, matrix products, shards(): jnp.einsum('tqf,tfh->tqh', split_piece, gate_signs, preferred_element_typ...  9.14 us
  transfers between devices with their start and end apart: 7, of which 7 were waited for; matrix products, arithmetic and copies ran while one was open for 5% of the time, Pallas kernels for 0%

commit v1 on v0

--- a/solution.py
+++ b/solution.py
@@ -148,7 +148,11 @@
     ).reshape(tokens, -1)
     summed_heads = lax.psum(projected.astype(jnp.bfloat16), "kv").astype(jnp.float32)
     hidden = residual[sort_order].astype(jnp.float32) + summed_heads
-    squares = lax.psum(jnp.sum(hidden * hidden, axis=1), "ctx")
+
+    def start_the_map(obj):
+        return jnp.sum(lax.all_gather(obj, "ctx"), axis=0)
+
+    squares = start_the_map(jnp.sum(hidden * hidden, axis=1))
     normed = (hidden * lax.rsqrt(squares / D + EPS)[:, None] * norm_gain).astype(jnp.bfloat16)
     hidden_units = gate_weight.shape[1]
     piece = lax.all_gather(normed, "ctx", axis=1, tiled=True)

time: 309 us -> 309 us (level)
    psum x1 -> x0, blocking collectives: 32.7 us -> none  [shards(): squares = lax.psum(jnp.sum(hidden * hidden, axis=1), 'ctx')]
    unnamed x0 -> x1, blocking collectives: none -> 32.7 us
where the time goes in v1:
time: 309 us
  waiting for transfers between devices  152 us (49%)
  blocking collectives  56.7 us (18%)
  matrix products  39 us (13%)
  local copies, waits for them, and re-layouts  17.5 us (6%)
  starting transfers between devices  16.6 us (5%)
  between operations  14.4 us (5%)
  other arithmetic  12.1 us (4%)
    reduce_scatter x1, waiting for transfers between devices, shards(): lax.psum_scatter(base_part + delta_part.reshape(features_here * lax.axis_...  59.5 us
    all_gather x1, waiting for transfers between devices, shards(): piece = lax.all_gather(normed, 'ctx', axis=1, tiled=True)  32.9 us
    unnamed x1, blocking collectives  32.7 us
    all_gather x1, blocking collectives, shards(): lax.all_gather(finished, 'ctx', axis=0, tiled=True)  24 us
    psum x1, waiting for transfers between devices, shards(): lowered = lax.psum(lowered.astype(jnp.bfloat16), 'kv').astype(jnp.float32)  20.4 us
    all_to_all x1, waiting for transfers between devices, shards(): lax.all_to_all(part_out.reshape(1, all_rows, HEAD_SIZE), 'ctx', split_axi...  17.5 us
    psum x1, waiting for transfers between devices, shards(): lax.psum(projected.astype(jnp.bfloat16), 'kv').astype(jnp.float32)  16.2 us
    dot_general x1, matrix products, shards(): jnp.einsum('tqf,tfh->tqh', split_piece, gate_signs, preferred_element_typ...  9.14 us
  transfers between devices with their start and end apart: 7, of which 7 were waited for; matrix products, arithmetic and copies ran while one was open for 5% of the time, Pallas kernels for 0%

profile of v1, /device:TPU:0, one launch (start us, length us, event | category | flops | bytes accessed | tf_op | source)
XLA Modules:
  0.0 308.8 jit_solution(13892788078501685625)
XLA Ops:
  6.5 2.8 sort.34
  11.7 1.9 copy-done.3
  15.7 7.4 %all-to-all-start.2 = ((f32[1,16,128]{2,0,1:T(1,128)}), f32[1,16,128]{2,0,1:T(1,128)S(1)}, u32[]{:S(2)}, u32[]{:S(2)}) async-start(f32[1,16,128]{2,0,1:T(1,128)} %bitcast.17), calls=%async_computation.2 | async-start | bytes 16384 | tf_op jit(solution)/shard_map/all_to_all | solution.py:112
  24.2 3.6 %fusion.9 = f32[2,32,4,8,128]{4,3,1,2,0:T(8,128)S(1)} fusion(f32[2,4,32,8,512]{4,3,2,1,0:T(8,128)} %copy-done.3, f32[2,32,4,8]{3,1,2,0:T(8,128)S(1)} %get-tuple-element.20, pred[2,512]{1,0:T(4,128)(4,1)S(1)} %broadcast_compare_fusion, bf16[2,512,4,128,1]{3,2,1,0,4:T(4,128)(2,1)} %bitcast.113), kind=kOutput, calls=%fused_computation.21 | convolution fusion | flops 273678336 | bytes 6300672 | tf_op jit(solution)/shard_map/tqgwj,tjgd->tqgwd/dot_general | solution.py:96
  29.4 5.2 %all-to-all-start.1 = ((f32[1,16,128]{2,0,1:T(1,128)}), f32[1,16,128]{2,0,1:T(1,128)S(1)}, u32[]{:S(2)}, u32[]{:S(2)}) async-start(f32[1,16,128]{2,0,1:T(1,128)} %bitcast.7), calls=%async_computation.1 | async-start | bytes 16384 | tf_op jit(solution)/shard_map/all_to_all | solution.py:109
  36.1 5.0 %all-to-all-done.1 = f32[1,16,128]{2,0,1:T(1,128)S(1)} async-done(((f32[1,16,128]{2,0,1:T(1,128)}), f32[1,16,128]{2,0,1:T(1,128)S(1)}, u32[]{:S(2)}, u32[]{:S(2)}) %all-to-all-start.1) | async-done | bytes 8224 | tf_op jit(solution)/shard_map/all_to_all | solution.py:109
  41.1 3.7 %all-to-all-start = ((f32[1,2048,128]{2,0,1:T(1,128)}), f32[1,2048,128]{2,0,1:T(1,128)S(1)}, u32[]{:S(2)}, u32[]{:S(2)}) async-start(f32[1,2048,128]{2,0,1:T(1,128)} %bitcast.5), calls=%async_computation | async-start | bytes 2097152 | tf_op jit(solution)/shard_map/all_to_all | solution.py:115
  50.1 17.5 %all-to-all-done = f32[1,2048,128]{2,0,1:T(1,128)S(1)} async-done(((f32[1,2048,128]{2,0,1:T(1,128)}), f32[1,2048,128]{2,0,1:T(1,128)S(1)}, u32[]{:S(2)}, u32[]{:S(2)}) %all-to-all-start) | async-done | bytes 1048608 | tf_op jit(solution)/shard_map/all_to_all | solution.py:115
  68.1 24.0 %all_gather.12 = bf16[2048,128]{1,0:T(8,128)(2,1)S(1)} all-gather(bf16[128,128]{1,0:T(8,128)(2,1)S(1)} %divide_convert_fusion), channel_id=1, replica_groups=mesh['kv'=2,'ctx'=16] {'ctx'}, dimensions={0}, use_global_device_ids=true | all-gather | bytes 557056 | tf_op jit(solution)/shard_map/all_gather | solution.py:138
  92.6 5.1 %convolution_multiply_fusion.1 = f32[2,32,512]{2,1,0:T(8,128)S(1)} fusion(bf16[2,32,4096]{2,1,0:T(8,128)(2,1)S(1)} %reshape_reshape.9, bf16[2,4096,512]{2,1,0:T(8,128)(2,1)} %param.29, f32[2]{0:T(128)S(1)} %get-tuple-element.11), kind=kOutput, calls=%fused_computation.22 | convolution fusion | flops 268468224 | bytes 9043976 | tf_op jit(solution)/shard_map/tqh,thf->tqf/dot_general | solution.py:143
  101.3 16.2 %all-reduce.4.cloned.1.call-done = bf16[64,512]{1,0:T(8,128)(2,1)} async-done(((bf16[64,512]{1,0:T(8,128)(2,1)}), bf16[64,512]{1,0:T(8,128)(2,1)}) %all-reduce.4.cloned.1.call-update) | async-done | bytes 65552 | tf_op jit(solution)/shard_map/psum | solution.py:149
  118.8 32.7 %all-reduce = f32[1024]{0:T(1024)S(1)} all-reduce(f32[1024]{0:T(1024)S(1)} %dynamic-update-slice), channel_id=2, replica_groups=mesh['kv'=2,'ctx'=16] {'ctx'}, use_global_device_ids=true, to_apply=%add | all-reduce | flops 1024 | bytes 8192
  151.5 1.6 multiply_convert_fusion
  153.4 32.9 %all-gather.3.cloned.1.call-done = bf16[64,8192]{1,0:T(8,128)(2,1)} async-done(((bf16[64,512]{1,0:T(8,128)(2,1)}), bf16[64,8192]{1,0:T(8,128)(2,1)}) %all-gather.3.cloned.1.call-update) | async-done | bytes 1048592 | tf_op jit(solution)/shard_map/all_gather | solution.py:158
  186.2 9.1 %convolution_multiply_fusion.3 = f32[2,32,512]{2,1,0:T(8,128)S(1)} fusion(bf16[2,32,8192]{2,1,0:T(8,128)(2,1)} %bitcast.94, bf16[2,8192,512]{2,1,0:T(8,128)(2,1)} %param.34, f32[2]{0:T(128)S(1)} %get-tuple-element.10), kind=kOutput, calls=%fused_computation.27 | convolution fusion | flops 536903680 | bytes 17956872 | tf_op jit(solution)/shard_map/tqf,tfh->tqh/dot_general | solution.py:163
  195.5 8.8 %convolution_multiply_fusion.2 = f32[2,32,512]{2,1,0:T(8,128)S(1)} fusion(bf16[2,32,8192]{2,1,0:T(8,128)(2,1)S(1)} %bitcast.95, bf16[2,8192,512]{2,1,0:T(8,128)(2,1)} %param.35, f32[2]{0:T(128)S(1)} %get-tuple-element.12), kind=kOutput, calls=%fused_computation.24 | convolution fusion | flops 536903680 | bytes 17956872 | tf_op jit(solution)/shard_map/tqf,tfh->tqh/dot_general | solution.py:166
  204.4 1.6 convolution_add_fusion.2
  206.0 1.6 fusion.15
  210.4 3.0 convolution_multiply_fusion
  213.4 2.9 fusion
  216.5 2.0 sort.35
  218.5 59.5 %reduce-scatter.2.cloned.1.call-done = f32[512,64]{0,1:T(8,128)} async-done(((f32[8192,64]{0,1:T(8,128)}), f32[512,64]{0,1:T(8,128)}) %reduce-scatter.2.cloned.1.call-update) | async-done | bytes 131088 | tf_op jit(solution)/shard_map/reduce_scatter | solution.py:184
  278.0 1.5 convert_bitcast_fusion
  279.6 20.4 %all-reduce.6.cloned.1.call-done = bf16[64,512]{1,0:T(8,128)(2,1)} async-done(((bf16[64,512]{1,0:T(8,128)(2,1)}), bf16[64,512]{1,0:T(8,128)(2,1)}) %all-reduce.6.cloned.1.call-update) | async-done | bytes 65552 | tf_op jit(solution)/shard_map/psum | solution.py:190
  (122 shorter events, 24.4 us)
Async XLA Ops:
  10.7 12.3 %copy-start.10 = (bf16[2,512,512]{2,1,0:T(8,128)(2,1)S(1)}, bf16[2,512,512]{2,1,0:T(8,128)(2,1)}, u32[]{:S(2)}) copy-start(bf16[2,512,512]{2,1,0:T(8,128)(2,1)} %param.24) | copy-start | bytes 3145732
  15.7 13.8 %all-to-all-start.2 = ((f32[1,16,128]{2,0,1:T(1,128)}), f32[1,16,128]{2,0,1:T(1,128)S(1)}, u32[]{:S(2)}, u32[]{:S(2)}) async-start(f32[1,16,128]{2,0,1:T(1,128)} %bitcast.17), calls=%async_computation.2 | async-start | bytes 16384 | tf_op jit(solution)/shard_map/all_to_all | solution.py:112
  27.8 17.2 %copy-start.5 = (bf16[64,512]{1,0:T(8,128)(2,1)S(1)}, bf16[64,512]{1,0:T(8,128)(2,1)}, u32[]{:S(2)}) copy-start(bf16[64,512]{1,0:T(8,128)(2,1)} %param.21) | copy-start | bytes 196612
  27.8 17.9 %copy-start.8 = (s32[64,64]{1,0:T(8,128)S(1)}, s32[64,64]{1,0:T(8,128)}, u32[]{:S(2)}) copy-start(s32[64,64]{1,0:T(8,128)} %param.26) | copy-start | bytes 49156
  27.8 20.1 %copy-start.6 = (bf16[64,512]{1,0:T(8,128)(2,1)S(1)}, bf16[64,512]{1,0:T(8,128)(2,1)}, u32[]{:S(2)}) copy-start(bf16[64,512]{1,0:T(8,128)(2,1)} %param.22) | copy-start | bytes 196612
  27.8 20.8 %copy-start.12 = (f32[2,4]{1,0:T(2,128)S(1)}, f32[2,4]{1,0:T(2,128)}, u32[]{:S(2)}) copy-start(f32[2,4]{1,0:T(2,128)} %param.37) | copy-start | bytes 100
  29.4 11.7 %all-to-all-start.1 = ((f32[1,16,128]{2,0,1:T(1,128)}), f32[1,16,128]{2,0,1:T(1,128)S(1)}, u32[]{:S(2)}, u32[]{:S(2)}) async-start(f32[1,16,128]{2,0,1:T(1,128)} %bitcast.7), calls=%async_computation.1 | async-start | bytes 16384 | tf_op jit(solution)/shard_map/all_to_all | solution.py:109
  41.1 26.5 %all-to-all-start = ((f32[1,2048,128]{2,0,1:T(1,128)}), f32[1,2048,128]{2,0,1:T(1,128)S(1)}, u32[]{:S(2)}, u32[]{:S(2)}) async-start(f32[1,2048,128]{2,0,1:T(1,128)} %bitcast.5), calls=%async_computation | async-start | bytes 2097152 | tf_op jit(solution)/shard_map/all_to_all | solution.py:115
  44.8 72.7 %all-reduce.4.cloned.1.call-start = ((), (), s32[]{:S(2)}) async-start(), calls=%async_computation.4 | async-start | bytes 131072 | tf_op jit(solution)/shard_map/psum | solution.py:149
  92.5 5.1 %copy-start.4 = (bf16[4096,512]{1,0:T(8,128)(2,1)S(1)}, bf16[4096,512]{1,0:T(8,128)(2,1)}, u32[]{:S(2)}) copy-start(bf16[4096,512]{1,0:T(8,128)(2,1)} %param.28) | copy-start | bytes 12582916
  97.6 53.9 %copy-start.13 = (f32[512]{0:T(512)S(1)}, f32[512]{0:T(512)}, u32[]{:S(2)}) copy-start(f32[512]{0:T(512)} %param.30) | copy-start | bytes 6148
  99.1 87.1 %all-gather.3.cloned.1.call-start = ((), (), s32[]{:S(2)}) async-start(), calls=%async_computation.5 | async-start | bytes 1114112 | tf_op jit(solution)/shard_map/all_gather | solution.py:158
  153.1 124.9 %reduce-scatter.2.cloned.1.call-start = ((), (), s32[]{:S(2)}) async-start(), calls=%async_computation.6 | async-start | bytes 2228224 | tf_op jit(solution)/shard_map/reduce_scatter | solution.py:184
  186.2 9.2 %copy-start.2 = (bf16[64,8192]{1,0:T(8,128)(2,1)S(1)}, bf16[64,8192]{1,0:T(8,128)(2,1)}, u32[]{:S(2)}) copy-start(bf16[64,8192]{1,0:T(8,128)(2,1)} %all-gather.3.cloned.1.call-done) | copy-start | bytes 3145732
  186.2 18.1 %slice-start = ((s8[8388608]{0:T(1024)(128)(4,1)}), s8[4194304]{0:T(1024)(128)(4,1)S(1)}, s32[]{:S(2)}) async-start(s8[8388608]{0:T(1024)(128)(4,1)} %bitcast.96), calls=%async_computation.8 | async-start | bytes 8388608
  186.2 19.7 %slice-start.2 = ((s8[8388608]{0:T(1024)(128)(4,1)}), s8[4194304]{0:T(1024)(128)(4,1)S(1)}, s32[]{:S(2)}) async-start(s8[8388608]{0:T(1024)(128)(4,1)} %bitcast.98), calls=%async_computation.10 | async-start | bytes 8388608
  195.4 8.9 %slice-start.1 = ((s8[8388608]{0:T(1024)(128)(4,1)}), s8[4194304]{0:T(1024)(128)(4,1)S(1)}, s32[]{:S(2)}) async-start(s8[8388608]{0:T(1024)(128)(4,1)} %bitcast.96), calls=%async_computation.9 | async-start | bytes 8388608
  195.4 10.5 %slice-start.3 = ((s8[8388608]{0:T(1024)(128)(4,1)}), s8[4194304]{0:T(1024)(128)(4,1)S(1)}, s32[]{:S(2)}) async-start(s8[8388608]{0:T(1024)(128)(4,1)} %bitcast.98), calls=%async_computation.11 | async-start | bytes 8388608
  204.4 4.6 %slice-start.8 = ((s8[16777216]{0:T(1024)(128)(4,1)}), s8[4194304]{0:T(1024)(128)(4,1)S(1)}, s32[]{:S(2)}) async-start(s8[16777216]{0:T(1024)(128)(4,1)} %bitcast.103), calls=%async_computation.16 | async-start | bytes 8388608
  206.0 4.4 %slice-start.9 = ((s8[16777216]{0:T(1024)(128)(4,1)}), s8[4194304]{0:T(1024)(128)(4,1)S(1)}, s32[]{:S(2)}) async-start(s8[16777216]{0:T(1024)(128)(4,1)} %bitcast.103), calls=%async_computation.17 | async-start | bytes 8388608
  206.0 7.4 %slice-start.4 = ((s8[8388608]{0:T(1024)(128)(4,1)}), s8[4194304]{0:T(1024)(128)(4,1)S(1)}, s32[]{:S(2)}) async-start(s8[8388608]{0:T(1024)(128)(4,1)} %bitcast.100), calls=%async_computation.12 | async-start | bytes 8388608
  213.4 86.6 %copy-start.11 = (bf16[64,512]{1,0:T(8,128)(2,1)S(1)}, bf16[64,512]{1,0:T(8,128)(2,1)}, u32[]{:S(2)}) copy-start(bf16[64,512]{1,0:T(8,128)(2,1)} %all-reduce.4.cloned.1.call-done) | copy-start | bytes 196612
  213.4 88.8 %copy-start.1 = (bf16[64,4096]{1,0:T(8,128)(2,1)S(1)}, bf16[64,4096]{1,0:T(8,128)(2,1)}, u32[]{:S(2)}) copy-start(bf16[64,4096]{1,0:T(8,128)(2,1)} %param.20) | copy-start | bytes 1572868
  216.4 83.7 %all-reduce.6.cloned.1.call-start = ((), (), s32[]{:S(2)}) async-start(), calls=%async_computation.7 | async-start | bytes 131072 | tf_op jit(solution)/shard_map/psum | solution.py:190
  (9 other events, 26.3 us)
Sparse Core Ops, SparseCore 0:
  99.3 18.2 all-reduce.3
  153.2 32.9 all-gather.2
  216.5 61.4 reduce-scatter.1
  280.1 19.8 all-reduce.5
